TPU v7x, 32 devices: a whole 2x2x4 slice. The times are simulated.
32 devices in a mesh: groups: 2 (over x), band: 16 (over z, y, core).
Axes of the slice: x: 2, y: 2, z: 4, core: 2. Of those that a mesh axis runs over, the one named last changes fastest.
Arguments:
- images: float32 [32, 8, 16, 32, 128], P(('groups', 'band')), parts along dimension 0, may hold values from -6 to 6
- coeffs: float32 [32, 8, 27, 3], P(('groups', 'band')), parts along dimension 0, may hold values from -3 to 3
- weights: float32 [32, 8], P(('groups', 'band')), parts along dimension 0, may hold values from 0.25 to 4
- scales: float32 [32, 8], P(('groups', 'band')), parts along dimension 0, may hold values from 0.5 to 2
- valid_epoch: int32 [32, 8], P(('groups', 'band')), parts along dimension 0, may hold values 0 or 1
- patch_owner: int32 [32, 8, 16, 1], P(('groups', 'band')), parts along dimension 0, may hold values from 0 to 15; in each aligned block of 128 rows (0 to 127, 128 to 255, ..., all dimensions but the last counted through in order) at most 16 rows name the same one
- patch_local: int32 [32, 8, 16], P(('groups', 'band')), parts along dimension 0, may hold values from 0 to 3
Outputs:
- difference: float32 [32, 8, 16, 32, 128], P(('groups', 'band')), parts along dimension 0
- templates: bfloat16 [128, 32, 128], P(('groups', 'band')), parts along dimension 0
There are 2 independent parts, one for each index of `groups`. A program takes and returns all parts, laid end to end along the dimension named above; each array names one. Nothing has to cross between parts.
Inputs may be any that keep to these rules, and one draw needn't show every extreme that they name: `patch_owner`: no band sends more than 16 of its tiles to one owner, and some band sends exactly 16 tiles to some owner; every owner receives some tile.
All inputs are finite; a program needn't handle non-finite values. No bound on the sum of `valid_epoch` on one device may be relied on, other than what follows from the above.
Results may differ from a plain program's by a relative error of at most 0.0078.
Values may be sent and summed in bfloat16 or wider, within the bound.
No kernel may reach another device: no remote copies, remote signals or barrier semaphores. Data moves between devices by JAX's collectives and lax.ppermute only.
A program may use at most 64 MiB of HBM per device.

v0:
```python
import jax
import jax.numpy as jnp
import numpy as np
from jax import lax
from jax.sharding import PartitionSpec as P

PD = 4
HALF = 9
P_SIZE = 3
sigmas = (0.75, 1.5, 3.0)
degrees = (4, 2, 2)


def kernel_matrices(tile_side):
    rows_out = lax.broadcasted_iota(jnp.int32, (tile_side, tile_side), 0)
    rows_in = lax.broadcasted_iota(jnp.int32, (tile_side, tile_side), 1)
    offset = (rows_out - rows_in).astype(jnp.float32)
    inside = (jnp.abs(rows_out - rows_in) <= HALF).astype(jnp.float32)
    taps = jnp.arange(-HALF, HALF + 1).astype(jnp.float32)
    tables = []
    for width_sigma, degree in zip(sigmas, degrees):
        normal_total = jnp.sum(jnp.exp(-taps * taps / (2.0 * width_sigma * width_sigma)))
        envelope = (
            jnp.exp(-offset * offset / (2.0 * width_sigma * width_sigma)) * inside / normal_total
        )
        for power in range(degree + 1):
            tables.append(envelope * (offset / width_sigma) ** power)
    return jnp.stack(tables)


def basis_pairs():
    kernel_list = []
    base_index = 0
    for degree in degrees:
        for column_power in range(degree + 1):
            for row_power in range(degree + 1 - column_power):
                kernel_list.append((base_index + row_power, base_index + column_power))
        base_index = base_index + degree + 1
    return kernel_list


def row_selector():
    kernel_list = basis_pairs()
    row_count = sum((degree + 1 for degree in degrees))
    table = np.zeros((len(kernel_list), row_count), np.float32)
    for basis_index, kernel_pair in enumerate(kernel_list):
        table[basis_index, kernel_pair[0]] = 1.0
    return jnp.asarray(table, jnp.float32)


def coordinates(per_epoch, tile_rows, tile_side):
    tile_index = lax.broadcasted_iota(jnp.float32, (per_epoch, tile_side), 0)
    column = lax.broadcasted_iota(jnp.float32, (per_epoch, tile_side), 1)
    across = 2.0 * (tile_index * tile_side + column + 0.5) / (per_epoch * tile_side) - 1.0
    down = 2.0 * (jnp.arange(tile_rows).astype(jnp.float32) + 0.5) / tile_rows - 1.0
    return (across, down)


def body(images, coeffs, weights, scales, valid_epoch, patch_owner, patch_local):
    band_count = lax.axis_size("band")
    epochs = images.shape[1]
    per_epoch = images.shape[2]
    tile_rows = images.shape[3]
    tile_side = images.shape[4]
    pixel_count = tile_rows * tile_side
    tile_count = epochs * per_epoch
    capacity = max(2, 2 * tile_count // band_count)
    column_kernels = kernel_matrices(tile_side)
    row_tables = kernel_matrices(tile_rows).astype(jnp.bfloat16)
    kernel_list = basis_pairs()
    column_stack = jnp.stack([column_kernels[kernel_pair[1]] for kernel_pair in kernel_list])
    selector = row_selector()
    row_count = column_kernels.shape[0]
    across, down = coordinates(per_epoch, tile_rows, tile_side)

    def one_epoch(epoch_inputs):
        tile_stack, coef_epoch = epoch_inputs
        mixing = selector[:, :, None] * coef_epoch[:, None, :]
        combined = jnp.einsum(
            "bjp,box->jxpo", mixing, column_stack, precision=lax.Precision.HIGHEST
        )
        mixer = combined.reshape(row_count * tile_side, P_SIZE * tile_side).astype(jnp.bfloat16)
        pixels = tile_stack.astype(jnp.bfloat16)
        rowed = jnp.einsum(
            "jpy,tyx->tpjx", row_tables, pixels, preferred_element_type=jnp.float32
        ).astype(jnp.bfloat16)
        flat = rowed.reshape(per_epoch, tile_rows, row_count * tile_side)
        spatial = jnp.einsum("tpk,kq->tpq", flat, mixer, preferred_element_type=jnp.float32)
        spatial = spatial.reshape(per_epoch, tile_rows, P_SIZE, tile_side)
        return (
            spatial[:, :, 0, :]
            + across[:, None, :] * spatial[:, :, 1, :]
            + down[None, :, None] * spatial[:, :, 2, :]
        )

    homogenized = lax.map(one_epoch, (images[0], coeffs[0])).reshape(tile_count, pixel_count)
    owners = patch_owner[0].reshape(tile_count)
    local_patch = patch_local[0].reshape(tile_count)
    order_index = jnp.arange(tile_count)
    earlier = (owners[:, None] == owners[None, :]) & (order_index[None, :] < order_index[:, None])
    send_rank = jnp.sum(earlier.astype(jnp.int32), axis=1)
    send_slot = owners * capacity + send_rank
    slot_total = band_count * capacity
    epoch_weight = (weights[0] * valid_epoch[0].astype(jnp.float32)).astype(jnp.bfloat16)
    tile_weight = jnp.broadcast_to(epoch_weight[:, None], (epochs, per_epoch)).reshape(tile_count)
    placement_table = (local_patch[:, None] == jnp.arange(PD)[None, :]).astype(jnp.bfloat16)
    weight_table = (
        placement_table.astype(jnp.float32) * tile_weight.astype(jnp.float32)[:, None]
    ).astype(jnp.bfloat16)
    outgoing = (
        jnp.zeros((slot_total, pixel_count), jnp.bfloat16)
        .at[send_slot]
        .set(homogenized.astype(jnp.bfloat16))
    )
    out_place = jnp.zeros((slot_total, PD), jnp.bfloat16).at[send_slot].set(placement_table)
    out_weight = jnp.zeros((slot_total, PD), jnp.bfloat16).at[send_slot].set(weight_table)
    received, got_place, got_weight = (
        lax.all_to_all(
            outgoing.reshape(band_count, capacity, pixel_count),
            "band",
            split_axis=0,
            concat_axis=0,
            tiled=True,
        ),
        lax.all_to_all(
            out_place.reshape(band_count, capacity, PD),
            "band",
            split_axis=0,
            concat_axis=0,
            tiled=True,
        ),
        lax.all_to_all(
            out_weight.reshape(band_count, capacity, PD),
            "band",
            split_axis=0,
            concat_axis=0,
            tiled=True,
        ),
    )
    flat_weight = got_weight.reshape(slot_total, PD)
    numerator = jnp.einsum(
        "sq,sk->qk",
        flat_weight,
        received.reshape(slot_total, pixel_count),
        preferred_element_type=jnp.float32,
    )
    denominator = 1.0 + jnp.sum(flat_weight.astype(jnp.float32), axis=0)
    templates = (numerator / denominator[:, None]).astype(jnp.bfloat16)
    global_patch = owners * PD + local_patch
    shard_rows = lax.all_gather(templates, "band", axis=0, tiled=True)
    row_total = shard_rows.shape[0]
    chooser = (global_patch[:, None] == jnp.arange(row_total)[None, :]).astype(jnp.bfloat16)
    matched = jnp.dot(chooser, shard_rows, preferred_element_type=jnp.float32)
    tile_scale = jnp.broadcast_to(scales[0][:, None], (epochs, per_epoch)).reshape(tile_count)
    difference = homogenized - tile_scale[:, None] * matched
    return (
        difference.reshape(1, epochs, per_epoch, tile_rows, tile_side),
        templates.reshape(PD, tile_rows, tile_side),
    )


def solution(mesh):
    return jax.shard_map(
        body,
        mesh=mesh,
        in_specs=(
            P(("groups", "band"), None, None, None, None),
            P(("groups", "band"), None, None, None),
            P(("groups", "band"), None),
            P(("groups", "band"), None),
            P(("groups", "band"), None),
            P(("groups", "band"), None, None, None),
            P(("groups", "band"), None, None),
        ),
        out_specs=(
            P(("groups", "band"), None, None, None, None),
            P(("groups", "band"), None, None),
        ),
        check_vma=False,
    )
```

profile of v0, /device:TPU:0, one launch (start us, length us, event | category | flops | bytes accessed | tf_op | source)
XLA Modules:
  0.0 226.5 jit_solution(9913890451470285794)
XLA Ops:
  2.7 1.4 fusion.47
  6.4 7.5 %all-to-all-start = ((bf16[16,16,4]{1,2,0:T(4,128)(2,1)}), bf16[16,16,4]{1,2,0:T(4,128)(2,1)}, u32[]{:S(2)}, u32[]{:S(2)}) async-start(bf16[16,16,4]{1,2,0:T(4,128)(2,1)} %copy.53), calls=%async_computation | async-start | bytes 32768 | tf_op jit(solution)/shard_map/all_to_all | solution.py:132
  15.9 1.2 constant_dynamic-update-slice_fusion.10
  22.3 1.3 constant_dynamic-update-slice_fusion.6
  27.2 1.2 constant_dynamic-update-slice_fusion.2
  29.7 1.2 constant_dynamic-update-slice_fusion
  31.0 2.8 %bitcast_convert_fusion.3 = bf16[8,16,32,128]{3,2,1,0:T(8,128)(2,1)} fusion(f32[1,8,16,32,128]{4,3,2,1,0:T(8,128)} %param.10), kind=kLoop, calls=%fused_computation.143 | loop fusion | flops 524288 | bytes 3145728
  51.4 2.3 %copy.50 = f32[27,128,128]{2,0,1:T(8,128)} copy(f32[27,128,128]{2,1,0:T(8,128)S(1)} %constant_dynamic-update-slice_fusion.11) | data formatting | bytes 3538944
  53.8 85.4 %while.12 = (s32[]{:T(128)}, f32[8,16,32,128]{3,2,1,0:T(8,128)}, bf16[8,16,32,128]{3,2,1,0:T(8,128)(2,1)}, bf16[11,32,32]{2,1,0:T(8,128)(2,1)}, f32[8,27,3]{1,2,...) while((s32[]{:T(128)}, f32[8,16,32,128]{3,2,1,0:T(8,128)}, ...), condition=%wide.region_4.0_spmd.clone.clone, body=%wide.region_3.0_spmd.sunk.clone.clone.sunk | while | flops 776496128 | bytes 16842668 | solution.py:96
  54.9 1.5 fusion.69
  58.1 4.2 %fusion.68 = bf16[11,3,128,128]{3,0,2,1:T(8,128)(2,1)S(1)} fusion(f32[27,128,128]{2,0,1:T(8,128)} %get-tuple-element.184, f32[27,3]{0,1:T(4,128)} %dynamic-slice_bitcast_fusion.2, f32[27,11]{0,1:T(8,128)S(1)} %get-tuple-element.187), kind=kOutput, calls=%fused_computation.6.clone.1 | convolution fusion | flops 175719296 | bytes 2852328 | tf_op jit(solution)/shard_map/while/body/eval_jaxpr/bjp,box->jxpo/dot_general | solution.py:79
  65.6 1.5 fusion.69
  68.8 4.2 %fusion.68 = bf16[11,3,128,128]{3,0,2,1:T(8,128)(2,1)S(1)} fusion(f32[27,128,128]{2,0,1:T(8,128)} %get-tuple-element.184, f32[27,3]{0,1:T(4,128)} %dynamic-slice_bitcast_fusion.2, f32[27,11]{0,1:T(8,128)S(1)} %get-tuple-element.187), kind=kOutput, calls=%fused_computation.6.clone.1 | convolution fusion | flops 175719296 | bytes 2852328 | tf_op jit(solution)/shard_map/while/body/eval_jaxpr/bjp,box->jxpo/dot_general | solution.py:79
  76.3 1.5 fusion.69
  79.4 4.2 %fusion.68 = bf16[11,3,128,128]{3,0,2,1:T(8,128)(2,1)S(1)} fusion(f32[27,128,128]{2,0,1:T(8,128)} %get-tuple-element.184, f32[27,3]{0,1:T(4,128)} %dynamic-slice_bitcast_fusion.2, f32[27,11]{0,1:T(8,128)S(1)} %get-tuple-element.187), kind=kOutput, calls=%fused_computation.6.clone.1 | convolution fusion | flops 175719296 | bytes 2852328 | tf_op jit(solution)/shard_map/while/body/eval_jaxpr/bjp,box->jxpo/dot_general | solution.py:79
  87.0 1.5 fusion.69
  90.1 4.2 %fusion.68 = bf16[11,3,128,128]{3,0,2,1:T(8,128)(2,1)S(1)} fusion(f32[27,128,128]{2,0,1:T(8,128)} %get-tuple-element.184, f32[27,3]{0,1:T(4,128)} %dynamic-slice_bitcast_fusion.2, f32[27,11]{0,1:T(8,128)S(1)} %get-tuple-element.187), kind=kOutput, calls=%fused_computation.6.clone.1 | convolution fusion | flops 175719296 | bytes 2852328 | tf_op jit(solution)/shard_map/while/body/eval_jaxpr/bjp,box->jxpo/dot_general | solution.py:79
  97.6 1.5 fusion.69
  100.8 4.2 %fusion.68 = bf16[11,3,128,128]{3,0,2,1:T(8,128)(2,1)S(1)} fusion(f32[27,128,128]{2,0,1:T(8,128)} %get-tuple-element.184, f32[27,3]{0,1:T(4,128)} %dynamic-slice_bitcast_fusion.2, f32[27,11]{0,1:T(8,128)S(1)} %get-tuple-element.187), kind=kOutput, calls=%fused_computation.6.clone.1 | convolution fusion | flops 175719296 | bytes 2852328 | tf_op jit(solution)/shard_map/while/body/eval_jaxpr/bjp,box->jxpo/dot_general | solution.py:79
  108.3 1.5 fusion.69
  111.5 4.2 %fusion.68 = bf16[11,3,128,128]{3,0,2,1:T(8,128)(2,1)S(1)} fusion(f32[27,128,128]{2,0,1:T(8,128)} %get-tuple-element.184, f32[27,3]{0,1:T(4,128)} %dynamic-slice_bitcast_fusion.2, f32[27,11]{0,1:T(8,128)S(1)} %get-tuple-element.187), kind=kOutput, calls=%fused_computation.6.clone.1 | convolution fusion | flops 175719296 | bytes 2852328 | tf_op jit(solution)/shard_map/while/body/eval_jaxpr/bjp,box->jxpo/dot_general | solution.py:79
  119.0 1.5 fusion.69
  122.2 4.2 %fusion.68 = bf16[11,3,128,128]{3,0,2,1:T(8,128)(2,1)S(1)} fusion(f32[27,128,128]{2,0,1:T(8,128)} %get-tuple-element.184, f32[27,3]{0,1:T(4,128)} %dynamic-slice_bitcast_fusion.2, f32[27,11]{0,1:T(8,128)S(1)} %get-tuple-element.187), kind=kOutput, calls=%fused_computation.6.clone.1 | convolution fusion | flops 175719296 | bytes 2852328 | tf_op jit(solution)/shard_map/while/body/eval_jaxpr/bjp,box->jxpo/dot_general | solution.py:79
  129.7 1.5 fusion.69
  132.8 4.2 %fusion.68 = bf16[11,3,128,128]{3,0,2,1:T(8,128)(2,1)S(1)} fusion(f32[27,128,128]{2,0,1:T(8,128)} %get-tuple-element.184, f32[27,3]{0,1:T(4,128)} %dynamic-slice_bitcast_fusion.2, f32[27,11]{0,1:T(8,128)S(1)} %get-tuple-element.187), kind=kOutput, calls=%fused_computation.6.clone.1 | convolution fusion | flops 175719296 | bytes 2852328 | tf_op jit(solution)/shard_map/while/body/eval_jaxpr/bjp,box->jxpo/dot_general | solution.py:79
  139.2 5.7 %scatter_custom_fusion.1 = bf16[256,4096]{1,0:T(8,128)(2,1)} fusion(s32[128]{0:T(128)} %copy-done.12, f32[16,8,32,128]{3,2,1,0:T(8,128)} %bitcast.141, bf16[]{:T(256)} %constant.93.clone.1), kind=kCustom, calls=%fused_computation.38 | custom fusion | bytes 4194816 | tf_op jit(solution)/shard_map/scatter | solution.py:113
  144.9 6.2 %all-to-all-start.1 = ((bf16[16,16,4096]{2,1,0:T(8,128)(2,1)}), bf16[16,16,4096]{2,1,0:T(8,128)(2,1)}, u32[]{:S(2)}, u32[]{:S(2)}) async-start(bf16[16,16,4096]{2,1,0:T(8,128)(2,1)} %bitcast.7), calls=%async_computation.1 | async-start | bytes 4194304 | tf_op jit(solution)/shard_map/all_to_all | solution.py:118
  152.1 40.0 %all-to-all-done.1 = bf16[16,16,4096]{2,1,0:T(8,128)(2,1)} async-done(((bf16[16,16,4096]{2,1,0:T(8,128)(2,1)}), bf16[16,16,4096]{2,1,0:T(8,128)(2,1)}, u32[]{:S(2)}, u32[]{:S(2)}) %all-to-all-start.1) | async-done | bytes 2097184 | tf_op jit(solution)/shard_map/all_to_all | solution.py:118
  192.1 2.0 fusion.27
  194.8 28.4 %all-gather = bf16[16,4,4096]{2,1,0:T(4,128)(2,1)S(1)} all-gather(bf16[1,4,4096]{2,1,0:T(4,128)(2,1)S(1)} %bitcast.145), channel_id=1, replica_groups=mesh['groups'=2,'band'=16] {'band'}, dimensions={0}, use_global_device_ids=true | all-gather | bytes 557056 | tf_op jit(solution)/shard_map/all_gather | solution.py:150
  223.4 1.5 fusion.28
  224.8 1.7 copy.65
  (221 shorter events, 75.1 us)
Async XLA Ops:
  1.4 3.2 %copy-start.7 = (s32[128]{0:T(128)}, s32[128]{0:T(128)S(1)}, u32[]{:S(2)}) copy-start(s32[128]{0:T(128)S(1)} %reshape_squeeze.7) | copy-start | bytes 1540
  4.7 11.1 %copy-start.12 = (s32[128]{0:T(128)}, s32[128]{0:T(128)S(1)}, u32[]{:S(2)}) copy-start(s32[128]{0:T(128)S(1)} %fusion.46) | copy-start | bytes 1540
  6.4 138.5 %all-to-all-start = ((bf16[16,16,4]{1,2,0:T(4,128)(2,1)}), bf16[16,16,4]{1,2,0:T(4,128)(2,1)}, u32[]{:S(2)}, u32[]{:S(2)}) async-start(bf16[16,16,4]{1,2,0:T(4,128)(2,1)} %copy.53), calls=%async_computation | async-start | bytes 32768 | tf_op jit(solution)/shard_map/all_to_all | solution.py:132
  51.4 2.4 %copy-start.1 = (f32[27,11]{0,1:T(8,128)S(1)}, f32[27,11]{0,1:T(8,128)}, u32[]{:S(2)}) copy-start(f32[27,11]{0,1:T(8,128)} %constant.97.clone..sunk.3) | copy-start | bytes 3568
  62.6 1.8 copy-start.3
  62.6 1.8 copy-start.6
  64.4 1.2 copy-start.5
  73.3 1.8 copy-start.3
  73.3 1.8 copy-start.6
  75.1 1.2 copy-start.5
  84.0 1.8 copy-start.3
  84.0 1.8 copy-start.6
  85.8 1.2 copy-start.5
  94.7 1.8 copy-start.3
  94.7 1.8 copy-start.6
  96.5 1.2 copy-start.5
  105.3 1.8 copy-start.3
  105.4 1.8 copy-start.6
  107.1 1.2 copy-start.5
  116.0 1.8 copy-start.3
  116.0 1.8 copy-start.6
  117.8 1.2 copy-start.5
  126.7 1.8 copy-start.3
  126.7 1.8 copy-start.6
  128.5 1.2 copy-start.5
  137.4 1.8 copy-start.3
  137.4 1.8 copy-start.6
  144.9 6.2 %copy-start.9 = (f32[1,8]{1,0:T(1,128)S(1)}, f32[1,8]{1,0:T(1,128)}, u32[]{:S(2)}) copy-start(f32[1,8]{1,0:T(1,128)} %param.13) | copy-start | bytes 100
  144.9 6.3 %copy-start.8 = (s32[128]{0:T(128)S(1)}, s32[128]{0:T(128)}, u32[]{:S(2)}) copy-start(s32[128]{0:T(128)} %copy-done.7) | copy-start | bytes 1540
  144.9 6.3 %copy-start.11 = (s32[128]{0:T(128)S(1)}, s32[128]{0:T(128)}, u32[]{:S(2)}) copy-start(s32[128]{0:T(128)} %copy-done.10) | copy-start | bytes 1540
  144.9 47.2 %all-to-all-start.1 = ((bf16[16,16,4096]{2,1,0:T(8,128)(2,1)}), bf16[16,16,4096]{2,1,0:T(8,128)(2,1)}, u32[]{:S(2)}, u32[]{:S(2)}) async-start(bf16[16,16,4096]{2,1,0:T(8,128)(2,1)} %bitcast.7), calls=%async_computation.1 | async-start | bytes 4194304 | tf_op jit(solution)/shard_map/all_to_all | solution.py:118
  152.1 71.2 %copy-start = (f32[8,16,32,128]{3,2,1,0:T(8,128)S(1)}, f32[8,16,32,128]{3,2,1,0:T(8,128)}, u32[]{:S(2)}) copy-start(f32[8,16,32,128]{3,2,1,0:T(8,128)} %get-tuple-element.49) | copy-start | bytes 6291460
  (18 other events, 19.0 us)
where the time goes:
time: 228 us; the launch traced here: 227 us
  matrix products  56.5 us (25%)
  other arithmetic  51.1 us (22%)
  waiting for transfers between devices  40 us (18%)
  local copies, waits for them, and re-layouts  35.3 us (15%)
  blocking collectives  28.4 us (12%)
  starting transfers between devices  13.6 us (6%)
    all_to_all x1, waiting for transfers between devices, body(): lax.all_to_all(outgoing.reshape(band_count, capacity, pixel_count), 'band...  40 us
    unnamed x38, other arithmetic  34 us
    dot_general x8, matrix products, one_epoch(): jnp.einsum('bjp,box->jxpo', mixing, column_stack, precision=lax.Precision...  33.7 us
    all_gather x1, blocking collectives, body(): shard_rows = lax.all_gather(templates, 'band', axis=0, tiled=True)  28.4 us
    dot_general x8, matrix products, one_epoch(): jnp.einsum('jpy,tyx->tpjx', row_tables, pixels, preferred_element_type=jn...  11.7 us
    reshape x8, local copies, waits for them, and re-layouts, one_epoch(): flat = rowed.reshape(per_epoch, tile_rows, row_count * tile_side)  7.69 us
    dot_general x8, matrix products, one_epoch(): jnp.einsum('tpk,kq->tpq', flat, mixer, preferred_element_type=jnp.float32)  7.57 us
    all_to_all x1, starting transfers between devices, body(): lax.all_to_all(out_weight.reshape(band_count, capacity, PD), 'band', spli...  7.46 us
  transfers between devices with their start and end apart: 2, of which 1 were waited for; matrix products, arithmetic and copies ran while one was open for 58% of the time, Pallas kernels for 0%

commit v1 on v0

--- a/solution.py
+++ b/solution.py
@@ -147,7 +147,12 @@
     denominator = 1.0 + jnp.sum(flat_weight.astype(jnp.float32), axis=0)
     templates = (numerator / denominator[:, None]).astype(jnp.bfloat16)
     global_patch = owners * PD + local_patch
-    shard_rows = lax.all_gather(templates, "band", axis=0, tiled=True)
+    ring = [templates]
+    for hop in range(15):
+        ring.append(lax.ppermute(ring[-1], "band", [(dev, (dev + 1) % 16) for dev in range(16)]))
+    shard_rows = jnp.roll(
+        jnp.concatenate(ring[::-1], axis=0), (lax.axis_index("band") + 1) * ring[0].shape[0], axis=0
+    )
     row_total = shard_rows.shape[0]
     chooser = (global_patch[:, None] == jnp.arange(row_total)[None, :]).astype(jnp.bfloat16)
     matched = jnp.dot(chooser, shard_rows, preferred_element_type=jnp.float32)

time: 228 us -> 300 us (1.32)
  waiting for transfers between devices: 40 us -> 134 us
  blocking collectives: 28.4 us -> 0 us
  local copies, waits for them, and re-layouts: 35.3 us -> 39.7 us
    ppermute x0 -> x15, waiting for transfers between devices: none -> 94.2 us  [body(): lax.ppermute(ring[-1], 'band', [(dev, (dev + 1) % 16) for dev in range(16)])]
    all_gather x1 -> x0, blocking collectives: 28.4 us -> none  [body(): shard_rows = lax.all_gather(templates, 'band', axis=0, tiled=True)]
    concatenate x0 -> x1, local copies, waits for them, and re-layouts: none -> 4.1 us  [body(): jnp.roll(jnp.concatenate(ring[::-1], axis=0), (lax.axis_index('band') + 1...]
    unnamed x22 -> x27, local copies, waits for them, and re-layouts: 6.17 us -> 6.02 us
  transfers between devices with their start and end apart: 2 -> 17, of which waited for: 1 -> 16; matrix products, arithmetic and copies ran while one was open for 58% -> 44% of each run, Pallas kernels for 0% -> 0%
where the time goes in v1:
time: 300 us; the launch traced here: 299 us
  waiting for transfers between devices  134 us (45%)
  matrix products  56.5 us (19%)
  other arithmetic  51.9 us (17%)
  local copies, waits for them, and re-layouts  39.7 us (13%)
  starting transfers between devices  14.5 us (5%)
    ppermute x15, waiting for transfers between devices, body(): lax.ppermute(ring[-1], 'band', [(dev, (dev + 1) % 16) for dev in range(16)])  94.2 us
    all_to_all x1, waiting for transfers between devices, body(): lax.all_to_all(outgoing.reshape(band_count, capacity, pixel_count), 'band...  40.1 us
    unnamed x38, other arithmetic  34.3 us
    dot_general x8, matrix products, one_epoch(): jnp.einsum('bjp,box->jxpo', mixing, column_stack, precision=lax.Precision...  33.7 us
    dot_general x8, matrix products, one_epoch(): jnp.einsum('jpy,tyx->tpjx', row_tables, pixels, preferred_element_type=jn...  11.7 us
    reshape x8, local copies, waits for them, and re-layouts, one_epoch(): flat = rowed.reshape(per_epoch, tile_rows, row_count * tile_side)  7.69 us
    dot_general x8, matrix products, one_epoch(): jnp.einsum('tpk,kq->tpq', flat, mixer, preferred_element_type=jnp.float32)  7.58 us
    all_to_all x1, starting transfers between devices, body(): lax.all_to_all(out_weight.reshape(band_count, capacity, PD), 'band', spli...  7.46 us
  transfers between devices with their start and end apart: 17, of which 16 were waited for; matrix products, arithmetic and copies ran while one was open for 44% of the time, Pallas kernels for 0%

profile of v1, /device:TPU:0, one launch (start us, length us, event | category | flops | bytes accessed | tf_op | source)
XLA Modules:
  0.0 298.6 jit_solution(16633729965661996397)
XLA Ops:
  6.4 7.5 %all-to-all-start = ((bf16[16,16,4]{1,2,0:T(4,128)(2,1)}), bf16[16,16,4]{1,2,0:T(4,128)(2,1)}, u32[]{:S(2)}, u32[]{:S(2)}) async-start(bf16[16,16,4]{1,2,0:T(4,128)(2,1)} %copy.45), calls=%async_computation | async-start | bytes 32768 | tf_op jit(solution)/shard_map/all_to_all | solution.py:132
  31.1 2.8 bitcast_convert_fusion.3
  51.8 2.3 copy.42
  54.1 86.3 %while.12 = (s32[]{:T(128)}, f32[8,16,32,128]{3,2,1,0:T(8,128)}, bf16[8,16,32,128]{3,2,1,0:T(8,128)(2,1)}, bf16[11,32,32]{2,1,0:T(8,128)(2,1)}, f32[8,27,3]{1,2,...) while((s32[]{:T(128)}, f32[8,16,32,128]{3,2,1,0:T(8,128)}, ...), condition=%wide.region_4.0_spmd.clone.clone, body=%wide.region_3.0_spmd.sunk.clone.clone.sunk | while | flops 776496128 | bytes 16842668 | solution.py:96
  58.5 4.2 %fusion.69 = bf16[11,3,128,128]{3,0,2,1:T(8,128)(2,1)S(1)} fusion(f32[27,128,128]{2,0,1:T(8,128)} %get-tuple-element.184, f32[27,3]{0,1:T(4,128)} %dynamic-slice_bitcast_fusion.2, f32[27,11]{0,1:T(8,128)S(1)} %get-tuple-element.187), kind=kOutput, calls=%fused_computation.6.clone.1 | convolution fusion | flops 175719296 | bytes 2852328 | tf_op jit(solution)/shard_map/while/body/eval_jaxpr/bjp,box->jxpo/dot_general | solution.py:79
  69.3 4.2 %fusion.69 = bf16[11,3,128,128]{3,0,2,1:T(8,128)(2,1)S(1)} fusion(f32[27,128,128]{2,0,1:T(8,128)} %get-tuple-element.184, f32[27,3]{0,1:T(4,128)} %dynamic-slice_bitcast_fusion.2, f32[27,11]{0,1:T(8,128)S(1)} %get-tuple-element.187), kind=kOutput, calls=%fused_computation.6.clone.1 | convolution fusion | flops 175719296 | bytes 2852328 | tf_op jit(solution)/shard_map/while/body/eval_jaxpr/bjp,box->jxpo/dot_general | solution.py:79
  80.1 4.2 %fusion.69 = bf16[11,3,128,128]{3,0,2,1:T(8,128)(2,1)S(1)} fusion(f32[27,128,128]{2,0,1:T(8,128)} %get-tuple-element.184, f32[27,3]{0,1:T(4,128)} %dynamic-slice_bitcast_fusion.2, f32[27,11]{0,1:T(8,128)S(1)} %get-tuple-element.187), kind=kOutput, calls=%fused_computation.6.clone.1 | convolution fusion | flops 175719296 | bytes 2852328 | tf_op jit(solution)/shard_map/while/body/eval_jaxpr/bjp,box->jxpo/dot_general | solution.py:79
  90.9 4.2 %fusion.69 = bf16[11,3,128,128]{3,0,2,1:T(8,128)(2,1)S(1)} fusion(f32[27,128,128]{2,0,1:T(8,128)} %get-tuple-element.184, f32[27,3]{0,1:T(4,128)} %dynamic-slice_bitcast_fusion.2, f32[27,11]{0,1:T(8,128)S(1)} %get-tuple-element.187), kind=kOutput, calls=%fused_computation.6.clone.1 | convolution fusion | flops 175719296 | bytes 2852328 | tf_op jit(solution)/shard_map/while/body/eval_jaxpr/bjp,box->jxpo/dot_general | solution.py:79
  101.7 4.2 %fusion.69 = bf16[11,3,128,128]{3,0,2,1:T(8,128)(2,1)S(1)} fusion(f32[27,128,128]{2,0,1:T(8,128)} %get-tuple-element.184, f32[27,3]{0,1:T(4,128)} %dynamic-slice_bitcast_fusion.2, f32[27,11]{0,1:T(8,128)S(1)} %get-tuple-element.187), kind=kOutput, calls=%fused_computation.6.clone.1 | convolution fusion | flops 175719296 | bytes 2852328 | tf_op jit(solution)/shard_map/while/body/eval_jaxpr/bjp,box->jxpo/dot_general | solution.py:79
  112.5 4.2 %fusion.69 = bf16[11,3,128,128]{3,0,2,1:T(8,128)(2,1)S(1)} fusion(f32[27,128,128]{2,0,1:T(8,128)} %get-tuple-element.184, f32[27,3]{0,1:T(4,128)} %dynamic-slice_bitcast_fusion.2, f32[27,11]{0,1:T(8,128)S(1)} %get-tuple-element.187), kind=kOutput, calls=%fused_computation.6.clone.1 | convolution fusion | flops 175719296 | bytes 2852328 | tf_op jit(solution)/shard_map/while/body/eval_jaxpr/bjp,box->jxpo/dot_general | solution.py:79
  123.3 4.2 %fusion.69 = bf16[11,3,128,128]{3,0,2,1:T(8,128)(2,1)S(1)} fusion(f32[27,128,128]{2,0,1:T(8,128)} %get-tuple-element.184, f32[27,3]{0,1:T(4,128)} %dynamic-slice_bitcast_fusion.2, f32[27,11]{0,1:T(8,128)S(1)} %get-tuple-element.187), kind=kOutput, calls=%fused_computation.6.clone.1 | convolution fusion | flops 175719296 | bytes 2852328 | tf_op jit(solution)/shard_map/while/body/eval_jaxpr/bjp,box->jxpo/dot_general | solution.py:79
  134.1 4.2 %fusion.69 = bf16[11,3,128,128]{3,0,2,1:T(8,128)(2,1)S(1)} fusion(f32[27,128,128]{2,0,1:T(8,128)} %get-tuple-element.184, f32[27,3]{0,1:T(4,128)} %dynamic-slice_bitcast_fusion.2, f32[27,11]{0,1:T(8,128)S(1)} %get-tuple-element.187), kind=kOutput, calls=%fused_computation.6.clone.1 | convolution fusion | flops 175719296 | bytes 2852328 | tf_op jit(solution)/shard_map/while/body/eval_jaxpr/bjp,box->jxpo/dot_general | solution.py:79
  140.4 5.8 %scatter_custom_fusion.1 = bf16[256,4096]{1,0:T(8,128)(2,1)} fusion(s32[128]{0:T(128)} %copy-done.15, f32[16,8,32,128]{3,2,1,0:T(8,128)} %bitcast.139, bf16[]{:T(256)} %constant.116.clone.1), kind=kCustom, calls=%fused_computation.38 | custom fusion | bytes 4194816 | tf_op jit(solution)/shard_map/scatter | solution.py:113
  146.2 6.0 %all-to-all-start.1 = ((bf16[16,16,4096]{2,1,0:T(8,128)(2,1)}), bf16[16,16,4096]{2,1,0:T(8,128)(2,1)}, u32[]{:S(2)}, u32[]{:S(2)}) async-start(bf16[16,16,4096]{2,1,0:T(8,128)(2,1)} %bitcast.7), calls=%async_computation.1 | async-start | bytes 4194304 | tf_op jit(solution)/shard_map/all_to_all | solution.py:118
  153.1 40.1 %all-to-all-done.1 = bf16[16,16,4096]{2,1,0:T(8,128)(2,1)} async-done(((bf16[16,16,4096]{2,1,0:T(8,128)(2,1)}), bf16[16,16,4096]{2,1,0:T(8,128)(2,1)}, u32[]{:S(2)}, u32[]{:S(2)}) %all-to-all-start.1) | async-done | bytes 2097184 | tf_op jit(solution)/shard_map/all_to_all | solution.py:118
  193.2 2.0 fusion.27
  196.2 10.5 %collective-permute-done = bf16[4,4096]{1,0:T(4,128)(2,1)S(1)} collective-permute-done((bf16[4,4096]{1,0:T(4,128)(2,1)S(1)}, bf16[4,4096]{1,0:T(4,128)(2,1)S(1)}, u32[]{:S(2)}, u32[]{:S(2)}) %collective-permute-start) | collective-permute-done | bytes 32800 | tf_op jit(solution)/shard_map/ppermute | solution.py:152
  206.7 6.0 %collective-permute-done.1 = bf16[4,4096]{1,0:T(4,128)(2,1)S(1)} collective-permute-done((bf16[4,4096]{1,0:T(4,128)(2,1)S(1)}, bf16[4,4096]{1,0:T(4,128)(2,1)S(1)}, u32[]{:S(2)}, u32[]{:S(2)}) %collective-permute-start.1) | collective-permute-done | bytes 32800 | tf_op jit(solution)/shard_map/ppermute | solution.py:152
  212.7 6.0 %collective-permute-done.2 = bf16[4,4096]{1,0:T(4,128)(2,1)S(1)} collective-permute-done((bf16[4,4096]{1,0:T(4,128)(2,1)S(1)}, bf16[4,4096]{1,0:T(4,128)(2,1)S(1)}, u32[]{:S(2)}, u32[]{:S(2)}) %collective-permute-start.2) | collective-permute-done | bytes 32800 | tf_op jit(solution)/shard_map/ppermute | solution.py:152
  218.8 6.0 %collective-permute-done.3 = bf16[4,4096]{1,0:T(4,128)(2,1)S(1)} collective-permute-done((bf16[4,4096]{1,0:T(4,128)(2,1)S(1)}, bf16[4,4096]{1,0:T(4,128)(2,1)S(1)}, u32[]{:S(2)}, u32[]{:S(2)}) %collective-permute-start.3) | collective-permute-done | bytes 32800 | tf_op jit(solution)/shard_map/ppermute | solution.py:152
  224.8 6.0 %collective-permute-done.4 = bf16[4,4096]{1,0:T(4,128)(2,1)S(1)} collective-permute-done((bf16[4,4096]{1,0:T(4,128)(2,1)S(1)}, bf16[4,4096]{1,0:T(4,128)(2,1)S(1)}, u32[]{:S(2)}, u32[]{:S(2)}) %collective-permute-start.4) | collective-permute-done | bytes 32800 | tf_op jit(solution)/shard_map/ppermute | solution.py:152
  230.9 6.0 %collective-permute-done.5 = bf16[4,4096]{1,0:T(4,128)(2,1)S(1)} collective-permute-done((bf16[4,4096]{1,0:T(4,128)(2,1)S(1)}, bf16[4,4096]{1,0:T(4,128)(2,1)S(1)}, u32[]{:S(2)}, u32[]{:S(2)}) %collective-permute-start.5) | collective-permute-done | bytes 32800 | tf_op jit(solution)/shard_map/ppermute | solution.py:152
  236.9 6.0 %collective-permute-done.6 = bf16[4,4096]{1,0:T(4,128)(2,1)S(1)} collective-permute-done((bf16[4,4096]{1,0:T(4,128)(2,1)S(1)}, bf16[4,4096]{1,0:T(4,128)(2,1)S(1)}, u32[]{:S(2)}, u32[]{:S(2)}) %collective-permute-start.6) | collective-permute-done | bytes 32800 | tf_op jit(solution)/shard_map/ppermute | solution.py:152
  242.9 6.0 %collective-permute-done.7 = bf16[4,4096]{1,0:T(4,128)(2,1)S(1)} collective-permute-done((bf16[4,4096]{1,0:T(4,128)(2,1)S(1)}, bf16[4,4096]{1,0:T(4,128)(2,1)S(1)}, u32[]{:S(2)}, u32[]{:S(2)}) %collective-permute-start.7) | collective-permute-done | bytes 32800 | tf_op jit(solution)/shard_map/ppermute | solution.py:152
  249.0 6.0 %collective-permute-done.8 = bf16[4,4096]{1,0:T(4,128)(2,1)S(1)} collective-permute-done((bf16[4,4096]{1,0:T(4,128)(2,1)S(1)}, bf16[4,4096]{1,0:T(4,128)(2,1)S(1)}, u32[]{:S(2)}, u32[]{:S(2)}) %collective-permute-start.8) | collective-permute-done | bytes 32800 | tf_op jit(solution)/shard_map/ppermute | solution.py:152
  255.0 6.0 %collective-permute-done.9 = bf16[4,4096]{1,0:T(4,128)(2,1)S(1)} collective-permute-done((bf16[4,4096]{1,0:T(4,128)(2,1)S(1)}, bf16[4,4096]{1,0:T(4,128)(2,1)S(1)}, u32[]{:S(2)}, u32[]{:S(2)}) %collective-permute-start.9) | collective-permute-done | bytes 32800 | tf_op jit(solution)/shard_map/ppermute | solution.py:152
  261.0 6.0 %collective-permute-done.10 = bf16[4,4096]{1,0:T(4,128)(2,1)S(1)} collective-permute-done((bf16[4,4096]{1,0:T(4,128)(2,1)S(1)}, bf16[4,4096]{1,0:T(4,128)(2,1)S(1)}, u32[]{:S(2)}, u32[]{:S(2)}) %collective-permute-start.10) | collective-permute-done | bytes 32800 | tf_op jit(solution)/shard_map/ppermute | solution.py:152
  267.1 6.0 %collective-permute-done.11 = bf16[4,4096]{1,0:T(4,128)(2,1)S(1)} collective-permute-done((bf16[4,4096]{1,0:T(4,128)(2,1)S(1)}, bf16[4,4096]{1,0:T(4,128)(2,1)S(1)}, u32[]{:S(2)}, u32[]{:S(2)}) %collective-permute-start.11) | collective-permute-done | bytes 32800 | tf_op jit(solution)/shard_map/ppermute | solution.py:152
  273.1 6.0 %collective-permute-done.12 = bf16[4,4096]{1,0:T(4,128)(2,1)S(1)} collective-permute-done((bf16[4,4096]{1,0:T(4,128)(2,1)S(1)}, bf16[4,4096]{1,0:T(4,128)(2,1)S(1)}, u32[]{:S(2)}, u32[]{:S(2)}) %collective-permute-start.12) | collective-permute-done | bytes 32800 | tf_op jit(solution)/shard_map/ppermute | solution.py:152
  279.2 6.0 %collective-permute-done.13 = bf16[4,4096]{1,0:T(4,128)(2,1)S(1)} collective-permute-done((bf16[4,4096]{1,0:T(4,128)(2,1)S(1)}, bf16[4,4096]{1,0:T(4,128)(2,1)S(1)}, u32[]{:S(2)}, u32[]{:S(2)}) %collective-permute-start.13) | collective-permute-done | bytes 32800 | tf_op jit(solution)/shard_map/ppermute | solution.py:152
  286.0 5.3 %collective-permute-done.14 = bf16[4,4096]{1,0:T(4,128)(2,1)} collective-permute-done((bf16[4,4096]{1,0:T(4,128)(2,1)S(1)}, bf16[4,4096]{1,0:T(4,128)(2,1)}, u32[]{:S(2)}, u32[]{:S(2)}) %collective-permute-start.14) | collective-permute-done | bytes 32800 | tf_op jit(solution)/shard_map/ppermute | solution.py:152
  291.3 4.1 %concatenate.6 = bf16[128,4096]{1,0:T(8,128)(2,1)S(1)} concatenate(bf16[4,4096]{1,0:T(4,128)(2,1)} %collective-permute-done.14, bf16[4,4096]{1,0:T(4,128)(2,1)} %copy-done.4, bf16[4,4096]{1,0:T(4,128)(2,1)} %copy-done.3, bf16[4,4096]{1,0:T(4,128)(2,1)} %copy-done.2, bf16[4,4096]{1,0:T(4,128)(2,1)S(1)} %collective-permute-done.10, bf16[4,4096]{1,0:T(4,128)(2,1)S(1)} %collective-permute-done.9, ...), dimensions={0} | concatenate | bytes 2097152 | tf_op jit(solution)/shard_map/jit(_roll_dynamic)/concatenate | solution.py:153
  (256 shorter events, 98.4 us)
Async XLA Ops:
  1.4 3.2 %copy-start.10 = (s32[128]{0:T(128)}, s32[128]{0:T(128)S(1)}, u32[]{:S(2)}) copy-start(s32[128]{0:T(128)S(1)} %reshape_squeeze.7) | copy-start | bytes 1540
  4.7 11.2 %copy-start.15 = (s32[128]{0:T(128)}, s32[128]{0:T(128)S(1)}, u32[]{:S(2)}) copy-start(s32[128]{0:T(128)S(1)} %fusion.47) | copy-start | bytes 1540
  6.4 139.8 %all-to-all-start = ((bf16[16,16,4]{1,2,0:T(4,128)(2,1)}), bf16[16,16,4]{1,2,0:T(4,128)(2,1)}, u32[]{:S(2)}, u32[]{:S(2)}) async-start(bf16[16,16,4]{1,2,0:T(4,128)(2,1)} %copy.45), calls=%async_computation | async-start | bytes 32768 | tf_op jit(solution)/shard_map/all_to_all | solution.py:132
  51.8 2.4 copy-start.1
  73.9 1.8 copy-start.6
  84.7 1.8 copy-start.6
  95.4 1.8 copy-start.6
  106.2 1.8 copy-start.6
  117.0 1.8 copy-start.6
  138.6 1.8 copy-start.6
  146.2 47.1 %all-to-all-start.1 = ((bf16[16,16,4096]{2,1,0:T(8,128)(2,1)}), bf16[16,16,4096]{2,1,0:T(8,128)(2,1)}, u32[]{:S(2)}, u32[]{:S(2)}) async-start(bf16[16,16,4096]{2,1,0:T(8,128)(2,1)} %bitcast.7), calls=%async_computation.1 | async-start | bytes 4194304 | tf_op jit(solution)/shard_map/all_to_all | solution.py:118
  152.2 133.0 %copy-start.11 = (s32[128]{0:T(128)S(1)}, s32[128]{0:T(128)}, u32[]{:S(2)}) copy-start(s32[128]{0:T(128)} %copy-done.10) | copy-start | bytes 1540
  152.2 133.0 %copy-start.14 = (s32[128]{0:T(128)S(1)}, s32[128]{0:T(128)}, u32[]{:S(2)}) copy-start(s32[128]{0:T(128)} %copy-done.13) | copy-start | bytes 1540
  152.2 133.0 %copy-start.12 = (f32[1,8]{1,0:T(1,128)S(1)}, f32[1,8]{1,0:T(1,128)}, u32[]{:S(2)}) copy-start(f32[1,8]{1,0:T(1,128)} %param.13) | copy-start | bytes 100
  153.1 142.4 %copy-start = (f32[8,16,32,128]{3,2,1,0:T(8,128)S(1)}, f32[8,16,32,128]{3,2,1,0:T(8,128)}, u32[]{:S(2)}) copy-start(f32[8,16,32,128]{3,2,1,0:T(8,128)} %get-tuple-element.49) | copy-start | bytes 6291460
  195.3 11.4 %collective-permute-start = (bf16[4,4096]{1,0:T(4,128)(2,1)S(1)}, bf16[4,4096]{1,0:T(4,128)(2,1)S(1)}, u32[]{:S(2)}, u32[]{:S(2)}) collective-permute-start(bf16[4,4096]{1,0:T(4,128)(2,1)S(1)} %fusion.27), channel_id=1, source_target_pairs={{0,1},{1,2},{2,3},{3,4},{4,5},{5,6},{6,7},{7,8},{8,9},{9,10},{10,1... | collective-permute-start | bytes 98312 | tf_op jit(solution)/shard_map/ppermute | solution.py:152
  206.7 6.0 %collective-permute-start.1 = (bf16[4,4096]{1,0:T(4,128)(2,1)S(1)}, bf16[4,4096]{1,0:T(4,128)(2,1)S(1)}, u32[]{:S(2)}, u32[]{:S(2)}) collective-permute-start(bf16[4,4096]{1,0:T(4,128)(2,1)S(1)} %collective-permute-done), channel_id=1, source_target_pairs={{0,1},{1,2},{2,3},{3,4},{4,5},{5,6},{6,7},{7,8},{8,9},{9,10},{10,1... | collective-permute-start | bytes 98312 | tf_op jit(solution)/shard_map/ppermute | solution.py:152
  212.7 6.0 %collective-permute-start.2 = (bf16[4,4096]{1,0:T(4,128)(2,1)S(1)}, bf16[4,4096]{1,0:T(4,128)(2,1)S(1)}, u32[]{:S(2)}, u32[]{:S(2)}) collective-permute-start(bf16[4,4096]{1,0:T(4,128)(2,1)S(1)} %collective-permute-done.1), channel_id=1, source_target_pairs={{0,1},{1,2},{2,3},{3,4},{4,5},{5,6},{6,7},{7,8},{8,9},{9,10},{10,1... | collective-permute-start | bytes 98312 | tf_op jit(solution)/shard_map/ppermute | solution.py:152
  218.8 6.0 %collective-permute-start.3 = (bf16[4,4096]{1,0:T(4,128)(2,1)S(1)}, bf16[4,4096]{1,0:T(4,128)(2,1)S(1)}, u32[]{:S(2)}, u32[]{:S(2)}) collective-permute-start(bf16[4,4096]{1,0:T(4,128)(2,1)S(1)} %collective-permute-done.2), channel_id=1, source_target_pairs={{0,1},{1,2},{2,3},{3,4},{4,5},{5,6},{6,7},{7,8},{8,9},{9,10},{10,1... | collective-permute-start | bytes 98312 | tf_op jit(solution)/shard_map/ppermute | solution.py:152
  224.8 6.0 %collective-permute-start.4 = (bf16[4,4096]{1,0:T(4,128)(2,1)S(1)}, bf16[4,4096]{1,0:T(4,128)(2,1)S(1)}, u32[]{:S(2)}, u32[]{:S(2)}) collective-permute-start(bf16[4,4096]{1,0:T(4,128)(2,1)S(1)} %collective-permute-done.3), channel_id=1, source_target_pairs={{0,1},{1,2},{2,3},{3,4},{4,5},{5,6},{6,7},{7,8},{8,9},{9,10},{10,1... | collective-permute-start | bytes 98312 | tf_op jit(solution)/shard_map/ppermute | solution.py:152
  230.9 6.0 %collective-permute-start.5 = (bf16[4,4096]{1,0:T(4,128)(2,1)S(1)}, bf16[4,4096]{1,0:T(4,128)(2,1)S(1)}, u32[]{:S(2)}, u32[]{:S(2)}) collective-permute-start(bf16[4,4096]{1,0:T(4,128)(2,1)S(1)} %collective-permute-done.4), channel_id=1, source_target_pairs={{0,1},{1,2},{2,3},{3,4},{4,5},{5,6},{6,7},{7,8},{8,9},{9,10},{10,1... | collective-permute-start | bytes 98312 | tf_op jit(solution)/shard_map/ppermute | solution.py:152
  236.9 6.0 %collective-permute-start.6 = (bf16[4,4096]{1,0:T(4,128)(2,1)S(1)}, bf16[4,4096]{1,0:T(4,128)(2,1)S(1)}, u32[]{:S(2)}, u32[]{:S(2)}) collective-permute-start(bf16[4,4096]{1,0:T(4,128)(2,1)S(1)} %collective-permute-done.5), channel_id=1, source_target_pairs={{0,1},{1,2},{2,3},{3,4},{4,5},{5,6},{6,7},{7,8},{8,9},{9,10},{10,1... | collective-permute-start | bytes 98312 | tf_op jit(solution)/shard_map/ppermute | solution.py:152
  242.9 6.0 %collective-permute-start.7 = (bf16[4,4096]{1,0:T(4,128)(2,1)S(1)}, bf16[4,4096]{1,0:T(4,128)(2,1)S(1)}, u32[]{:S(2)}, u32[]{:S(2)}) collective-permute-start(bf16[4,4096]{1,0:T(4,128)(2,1)S(1)} %collective-permute-done.6), channel_id=1, source_target_pairs={{0,1},{1,2},{2,3},{3,4},{4,5},{5,6},{6,7},{7,8},{8,9},{9,10},{10,1... | collective-permute-start | bytes 98312 | tf_op jit(solution)/shard_map/ppermute | solution.py:152
  249.0 6.0 %collective-permute-start.8 = (bf16[4,4096]{1,0:T(4,128)(2,1)S(1)}, bf16[4,4096]{1,0:T(4,128)(2,1)S(1)}, u32[]{:S(2)}, u32[]{:S(2)}) collective-permute-start(bf16[4,4096]{1,0:T(4,128)(2,1)S(1)} %collective-permute-done.7), channel_id=1, source_target_pairs={{0,1},{1,2},{2,3},{3,4},{4,5},{5,6},{6,7},{7,8},{8,9},{9,10},{10,1... | collective-permute-start | bytes 98312 | tf_op jit(solution)/shard_map/ppermute | solution.py:152
  255.0 6.0 %collective-permute-start.9 = (bf16[4,4096]{1,0:T(4,128)(2,1)S(1)}, bf16[4,4096]{1,0:T(4,128)(2,1)S(1)}, u32[]{:S(2)}, u32[]{:S(2)}) collective-permute-start(bf16[4,4096]{1,0:T(4,128)(2,1)S(1)} %collective-permute-done.8), channel_id=1, source_target_pairs={{0,1},{1,2},{2,3},{3,4},{4,5},{5,6},{6,7},{7,8},{8,9},{9,10},{10,1... | collective-permute-start | bytes 98312 | tf_op jit(solution)/shard_map/ppermute | solution.py:152
  261.0 6.0 %collective-permute-start.10 = (bf16[4,4096]{1,0:T(4,128)(2,1)S(1)}, bf16[4,4096]{1,0:T(4,128)(2,1)S(1)}, u32[]{:S(2)}, u32[]{:S(2)}) collective-permute-start(bf16[4,4096]{1,0:T(4,128)(2,1)S(1)} %collective-permute-done.9), channel_id=1, source_target_pairs={{0,1},{1,2},{2,3},{3,4},{4,5},{5,6},{6,7},{7,8},{8,9},{9,10},{10,1... | collective-permute-start | bytes 98312 | tf_op jit(solution)/shard_map/ppermute | solution.py:152
  267.1 6.0 %collective-permute-start.11 = (bf16[4,4096]{1,0:T(4,128)(2,1)S(1)}, bf16[4,4096]{1,0:T(4,128)(2,1)S(1)}, u32[]{:S(2)}, u32[]{:S(2)}) collective-permute-start(bf16[4,4096]{1,0:T(4,128)(2,1)S(1)} %collective-permute-done.10), channel_id=1, source_target_pairs={{0,1},{1,2},{2,3},{3,4},{4,5},{5,6},{6,7},{7,8},{8,9},{9,10},{10,1... | collective-permute-start | bytes 98312 | tf_op jit(solution)/shard_map/ppermute | solution.py:152
  273.1 12.9 %copy-start.2 = (bf16[4,4096]{1,0:T(4,128)(2,1)}, bf16[4,4096]{1,0:T(4,128)(2,1)S(1)}, u32[]{:S(2)}) copy-start(bf16[4,4096]{1,0:T(4,128)(2,1)S(1)} %collective-permute-done.11) | copy-start | bytes 98308
  273.1 6.0 %collective-permute-start.12 = (bf16[4,4096]{1,0:T(4,128)(2,1)S(1)}, bf16[4,4096]{1,0:T(4,128)(2,1)S(1)}, u32[]{:S(2)}, u32[]{:S(2)}) collective-permute-start(bf16[4,4096]{1,0:T(4,128)(2,1)S(1)} %collective-permute-done.11), channel_id=1, source_target_pairs={{0,1},{1,2},{2,3},{3,4},{4,5},{5,6},{6,7},{7,8},{8,9},{9,10},{10,1... | collective-permute-start | bytes 98312 | tf_op jit(solution)/shard_map/ppermute | solution.py:152
  279.2 6.9 %copy-start.3 = (bf16[4,4096]{1,0:T(4,128)(2,1)}, bf16[4,4096]{1,0:T(4,128)(2,1)S(1)}, u32[]{:S(2)}) copy-start(bf16[4,4096]{1,0:T(4,128)(2,1)S(1)} %collective-permute-done.12) | copy-start | bytes 98308
  279.2 6.0 %collective-permute-start.13 = (bf16[4,4096]{1,0:T(4,128)(2,1)S(1)}, bf16[4,4096]{1,0:T(4,128)(2,1)S(1)}, u32[]{:S(2)}, u32[]{:S(2)}) collective-permute-start(bf16[4,4096]{1,0:T(4,128)(2,1)S(1)} %collective-permute-done.12), channel_id=1, source_target_pairs={{0,1},{1,2},{2,3},{3,4},{4,5},{5,6},{6,7},{7,8},{8,9},{9,10},{10,1... | collective-permute-start | bytes 98312 | tf_op jit(solution)/shard_map/ppermute | solution.py:152
  285.2 6.1 %collective-permute-start.14 = (bf16[4,4096]{1,0:T(4,128)(2,1)S(1)}, bf16[4,4096]{1,0:T(4,128)(2,1)}, u32[]{:S(2)}, u32[]{:S(2)}) collective-permute-start(bf16[4,4096]{1,0:T(4,128)(2,1)S(1)} %collective-permute-done.13), channel_id=1, source_target_pairs={{0,1},{1,2},{2,3},{3,4},{4,5},{5,6},{6,7},{7,8},{8,9},{9,10},{10,1... | collective-permute-start | bytes 98312 | tf_op jit(solution)/shard_map/ppermute | solution.py:152
  (36 other events, 47.6 us)
